TPU v7x, 32 devices: a whole 2x2x4 slice. The times are simulated.
32 devices in a mesh: groups: 2 (over y), seq: 4 (over x, core), tensor: 4 (over z).
Axes of the slice: x: 2, y: 2, z: 4, core: 2. Of those that a mesh axis runs over, the one named last changes fastest.
Arguments:
- patches: bfloat16 [2056, 1280], P(('groups', 'seq')), parts along dimension 0, may hold values from -6 to 6
- latents: bfloat16 [64, 1280], replicated, may hold values from -160 to 160
- wq_res: bfloat16 [1280, 1536], P(None, 'tensor'), may hold values from -0.15625 to 0.15625
- wk_res: bfloat16 [1280, 1536], P(None, 'tensor'), may hold values from -0.3125 to 0.3125
- wv_res: bfloat16 [1280, 1536], P(None, 'tensor'), may hold values from -0.15625 to 0.15625
- wo_res: bfloat16 [1536, 1280], P('tensor'), may hold values from -0.625 to 0.625
- text: bfloat16 [3072, 8192], P('groups', 'seq'), parts along dimension 0, may hold values from -240 to 240
- norm_gain: bfloat16 [8192], P('seq'), may hold values from 0.25 to 1.75
- wq_x: bfloat16 [8192, 8192], P('seq', 'tensor'), may hold values from -0.0625 to 0.0625
- wk_x: bfloat16 [1280, 8192], P(None, 'tensor'), may hold values from -0.15625 to 0.15625
- wv_x: bfloat16 [1280, 8192], P(None, 'tensor'), may hold values from -0.15625 to 0.15625
- wo_x: bfloat16 [8192, 8192], P('tensor', 'seq'), may hold values from -0.25 to 0.25
- gate_x: float32 [8192], P('seq'), may hold values from -1.5 to 1.5
- text_image: int32 [3072], P('groups'), parts along dimension 0, may hold values from -1 to 3, as said below
Outputs:
- text_out: float32 [3072, 8192], P('groups', 'seq'), parts along dimension 0
- page_latents: bfloat16 [512, 1280], P(('groups', 'seq')), parts along dimension 0
There are 2 independent parts, one for each index of `groups`. A program takes and returns all parts, laid end to end along the dimension named above; an argument that names none is the same for every part. Nothing has to cross between parts.
Inputs may be any that keep to these rules, and one draw needn't show every extreme that they name: text_image[t] is the index of the last image placed at or before token t, -1 before the first image; it never falls along the tokens, and every one of the 4 images is the value of some tokens.
All inputs are finite; a program needn't handle non-finite values.
Results may differ from a plain program's by a relative error of at most 0.015.
The roundings to bfloat16 on the way count: a program that leaves them out, or rounds other values in their place, can miss the bound.
Values may be sent and summed in bfloat16 or wider, within the bound.
A program may use at most 192 MiB of HBM per device.

v0:
```python
import math
import jax
import jax.numpy as jnp
from jax import lax
from jax.sharding import PartitionSpec as P

WIDTH = 8192
HEAD = 128
RES_HEAD = 96
PATCH_IMG = 257


def shards(
    patches,
    latents,
    wq_res,
    wk_res,
    wv_res,
    wo_res,
    text,
    norm_gain,
    wq_x,
    wk_x,
    wv_x,
    wo_x,
    gate_x,
    text_image,
):
    inv_res = 1.0 / math.sqrt(RES_HEAD)
    inv_root = 1.0 / math.sqrt(HEAD)
    lat_count = latents.shape[0]
    img_count = patches.shape[0] // PATCH_IMG
    heads_res = wq_res.shape[1] // RES_HEAD
    queries = (
        jnp.dot(latents, wq_res, preferred_element_type=jnp.float32)
        .astype(jnp.bfloat16)
        .reshape(lat_count, heads_res, RES_HEAD)
    )
    page_keys = (
        jnp.dot(patches, wk_res, preferred_element_type=jnp.float32)
        .astype(jnp.bfloat16)
        .reshape(img_count, PATCH_IMG, heads_res, RES_HEAD)
    )
    page_values = (
        jnp.dot(patches, wv_res, preferred_element_type=jnp.float32)
        .astype(jnp.bfloat16)
        .reshape(img_count, PATCH_IMG, heads_res, RES_HEAD)
    )
    scores = (
        jnp.einsum("lhd,iphd->ihlp", queries, page_keys, preferred_element_type=jnp.float32)
        * inv_res
    )
    summit = jnp.max(scores, axis=3, keepdims=True)
    weights = jnp.exp(scores - summit).astype(jnp.bfloat16)
    totals = jnp.sum(weights, axis=3, dtype=jnp.float32)
    blended = jnp.einsum(
        "ihlp,iphd->ihld", weights, page_values, preferred_element_type=jnp.float32
    )
    pooled = (
        (blended / totals[:, :, :, None])
        .transpose(0, 2, 1, 3)
        .reshape(img_count * lat_count, heads_res * RES_HEAD)
        .astype(jnp.bfloat16)
    )
    partial_value = jnp.dot(pooled, wo_res, preferred_element_type=jnp.float32)
    latent_sum = lax.psum(partial_value, "tensor")
    repeated = jnp.tile(latents, (img_count, 1)).astype(jnp.float32)
    page_latents = (repeated + latent_sum).astype(jnp.bfloat16)
    tok_count = text.shape[0]
    hidden = text.astype(jnp.float32)
    squares = jnp.sum(hidden * hidden, axis=1)
    scaled = (hidden * norm_gain.astype(jnp.float32)).astype(jnp.bfloat16)
    query_part = jnp.dot(scaled, wq_x, preferred_element_type=jnp.float32)
    squares, query_sum = lax.psum((squares, query_part), "seq")
    inverse = lax.rsqrt(squares / WIDTH + 1e-05)
    heads_x = wq_x.shape[1] // HEAD
    text_queries = (query_sum * inverse[:, None]).astype(jnp.bfloat16)
    own_keys = jnp.dot(page_latents, wk_x, preferred_element_type=jnp.float32).astype(jnp.bfloat16)
    own_values = jnp.dot(page_latents, wv_x, preferred_element_type=jnp.float32).astype(
        jnp.bfloat16
    )
    cross_keys, cross_values = (
        lax.all_gather(own_keys, "seq", axis=0, tiled=True),
        lax.all_gather(own_values, "seq", axis=0, tiled=True),
    )
    lat_all = cross_keys.shape[0]
    cross_keys = cross_keys.reshape(lat_all, heads_x, HEAD)
    cross_values = cross_values.reshape(lat_all, heads_x, HEAD)
    latent_owner = jnp.arange(lat_all, dtype=jnp.int32) // lat_count
    row_block = math.gcd(tok_count, 512)
    n_blocks = tok_count // row_block
    q_blocks = text_queries.reshape(n_blocks, row_block, heads_x, HEAD)
    img_blocks = text_image.reshape(n_blocks, row_block)

    def attend(inputs):
        q_rows, img_rows = inputs
        logits = (
            jnp.einsum("thd,lhd->htl", q_rows, cross_keys, preferred_element_type=jnp.float32)
            * inv_root
        )
        allowed = img_rows[:, None] == latent_owner[None, :]
        logits = jnp.where(allowed[None, :, :], logits, -1e30)
        row_peak = jnp.max(logits, axis=2, keepdims=True)
        probs_bf = jnp.exp(logits - row_peak).astype(jnp.bfloat16)
        row_total = jnp.sum(probs_bf, axis=2, dtype=jnp.float32)
        mixture = jnp.einsum(
            "htl,lhd->thd", probs_bf, cross_values, preferred_element_type=jnp.float32
        )
        visible = (img_rows >= 0).astype(jnp.float32)
        return (mixture / row_total.T[:, :, None] * visible[:, None, None]).astype(jnp.bfloat16)

    attended = lax.map(attend, (q_blocks, img_blocks)).reshape(tok_count, heads_x * HEAD)
    block_part = jnp.dot(attended, wo_x, preferred_element_type=jnp.float32)
    gate_open = jnp.tanh(gate_x)
    block_whole = lax.psum(block_part.astype(jnp.bfloat16), "tensor").astype(jnp.float32)
    text_out = hidden + gate_open * block_whole
    return (text_out, page_latents)


def solution(mesh):
    in_specs = (
        P(("groups", "seq"), None),
        P(),
        P(None, "tensor"),
        P(None, "tensor"),
        P(None, "tensor"),
        P("tensor", None),
        P("groups", "seq"),
        P("seq"),
        P("seq", "tensor"),
        P(None, "tensor"),
        P(None, "tensor"),
        P("tensor", "seq"),
        P("seq"),
        P("groups"),
    )
    out_specs = (P("groups", "seq"), P(("groups", "seq"), None))
    return jax.shard_map(shards, mesh=mesh, in_specs=in_specs, out_specs=out_specs, check_vma=False)
```

profile of v0, /device:TPU:0, one launch (start us, length us, event | category | flops | bytes accessed | tf_op | source)
XLA Modules:
  0.0 635.0 jit_solution(5875707518718355605)
XLA Ops:
  7.2 1.4 copy-done
  8.7 1.6 convolution_convert_fusion.4
  10.3 0.3 reshape.96
  10.6 1.6 convolution_convert_fusion.5
  12.2 0.1 reshape.97
  12.3 1.9 convolution_convert_fusion.3
  14.2 0.3 reshape.99
  14.6 0.3 fusion.24
  14.9 0.2 convert_reduce_fusion.1
  15.1 0.3 fusion.19
  15.5 0.1 convert_element_type.86
  15.6 1.0 fusion.25
  16.7 39.3 %all-reduce.6.cloned.1.call-done = f32[64,1280]{1,0:T(8,128)} async-done(((f32[64,1280]{1,0:T(8,128)}), f32[64,1280]{1,0:T(8,128)}) %all-reduce.6.cloned.1.call-update) | async-done | bytes 327696 | tf_op jit(solution)/shard_map/psum | solution.py:66
  55.9 1.0 add_convert_fusion
  56.9 4.3 convolution_convert_fusion.1
  61.3 4.2 convolution_convert_fusion.2
  65.6 19.3 %fusion.12 = f32[1536,2048]{1,0:T(8,128)} fusion(bf16[2048,2048]{1,0:T(8,128)(2,1)} %param.24, bf16[1536,2048]{1,0:T(8,128)(2,1)} %param.22, f32[2048]{0:T(1024)S(1)} %convert_element_type.74), kind=kOutput, calls=%fused_computation.30 | convolution fusion | flops 12894339072 | bytes 27271168 | tf_op jit(solution)/shard_map/dot_general | solution.py:73
  84.9 0.6 copy-done.5
  85.6 4.3 fusion.10
  89.9 6.4 %psum.29 = f32[1536]{0:T(1024)S(1)} all-reduce(f32[1536]{0:T(1024)S(1)} %fusion.10), channel_id=1, replica_groups=mesh['groups'=2,'seq'=4,'tensor'=4] {'seq'}, use_global_device_ids=true, to_apply=%region_2.0 | all-reduce | flops 1536 | bytes 12288 | tf_op jit(solution)/shard_map/psum | solution.py:74
  96.3 1.5 copy_bitcast_fusion.2
  97.8 1.5 copy_bitcast_fusion.3
  99.3 220.7 %all-reduce.4.cloned.1.call-done = f32[1536,2048]{1,0:T(8,128)} async-done(((f32[1536,2048]{1,0:T(8,128)}), f32[1536,2048]{1,0:T(8,128)}) %all-reduce.4.cloned.1.call-update) | async-done | bytes 12582928 | tf_op jit(solution)/shard_map/psum | solution.py:74
  320.0 8.4 %fusion.11 = bf16[192,8,16,128]{3,1,2,0:T(8,128)(2,1)} fusion(f32[1536,2048]{1,0:T(8,128)} %all-reduce.4.cloned.1.call-done, f32[1536]{0:T(1024)S(1)} %add_rsqrt_fusion), kind=kLoop, calls=%fused_computation.29 | loop fusion | flops 6291456 | bytes 18880512
  328.4 7.8 %copy.38 = bf16[192,8,16,128]{3,2,1,0:T(8,128)(2,1)} copy(bf16[192,8,16,128]{3,1,2,0:T(8,128)(2,1)} %fusion.11) | data formatting | bytes 12582912
  336.1 37.6 %while.11 = (s32[]{:T(128)}, bf16[3,512,16,128]{3,2,1,0:T(8,128)(2,1)}, s32[3,512]{1,0:T(4,128)S(1)}, bf16[3,512,16,128]{3,2,1,0:T(8,128)(2,1)}, bf16[256,16,128...) while((s32[]{:T(128)}, bf16[3,512,16,128]{3,2,1,0:T(8,128)(2,1)}, ...), condition=%wide.region_9.10_spmd.clone, body=%wide.region_6.9_spmd.clone.sunk | while | flops 1104268288 | bytes 40548948 | solution.py:112
  336.2 0.1 broadcast_compare_fusion.2
  336.3 2.0 constant_dynamic-slice_fusion.5
  338.3 2.4 fusion.50
  340.7 1.8 convert_reduce_fusion.3
  342.5 3.5 fusion.51
  346.0 2.7 copy_dynamic-update-slice_fusion.2
  348.7 0.1 broadcast_compare_fusion.2
  348.9 2.0 constant_dynamic-slice_fusion.5
  350.8 2.4 fusion.50
  353.2 1.8 convert_reduce_fusion.3
  355.1 3.5 fusion.51
  358.5 2.7 copy_dynamic-update-slice_fusion.2
  361.2 0.1 broadcast_compare_fusion.2
  361.4 2.0 constant_dynamic-slice_fusion.5
  363.3 2.4 fusion.50
  365.7 1.8 convert_reduce_fusion.3
  367.6 3.5 fusion.51
  371.0 2.7 copy_dynamic-update-slice_fusion.2
  373.8 18.9 %convolution_convert_fusion = bf16[1536,2048]{1,0:T(8,128)(2,1)} fusion(bf16[2048,2048]{1,0:T(8,128)(2,1)} %param.27, bf16[192,8,16,128]{3,2,1,0:T(8,128)(2,1)} %bitcast.20), kind=kOutput, calls=%fused_computation.28 | convolution fusion | flops 12888047616 | bytes 20971520 | tf_op jit(solution)/shard_map/dot_general | solution.py:113
  392.7 0.7 copy-done.6
  393.3 222.5 %all-reduce.8.cloned.1.call-done = bf16[1536,2048]{1,0:T(8,128)(2,1)} async-done(((bf16[1536,2048]{1,0:T(8,128)(2,1)}), bf16[1536,2048]{1,0:T(8,128)(2,1)}) %all-reduce.8.cloned.1.call-update) | async-done | bytes 6291472 | tf_op jit(solution)/shard_map/psum | solution.py:115
  615.9 12.6 %convert_add_fusion = f32[1536,2048]{1,0:T(8,128)} fusion(bf16[1536,2048]{1,0:T(8,128)(2,1)} %param.22, bf16[1536,2048]{1,0:T(8,128)(2,1)} %all-reduce.8.cloned.1.call-done, f32[2048]{0:T(1024)S(1)} %tanh.3), kind=kLoop, calls=%fused_computation.22 | loop fusion | flops 12582912 | bytes 25174016 | tf_op jit(solution)/shard_map/add | solution.py:116
  (40 shorter events, 0.5 us)
Async XLA Ops:
  7.2 1.5 copy-start
  7.2 48.7 %copy-start.4 = (bf16[64,1280]{1,0:T(8,128)(2,1)S(1)}, bf16[64,1280]{1,0:T(8,128)(2,1)}, u32[]{:S(2)}) copy-start(bf16[64,1280]{1,0:T(8,128)(2,1)} %param.17) | copy-start | bytes 491524
  7.2 8.4 %copy-start.3 = (bf16[384,1280]{1,0:T(8,128)(2,1)S(1)}, bf16[384,1280]{1,0:T(8,128)(2,1)}, u32[]{:S(2)}) copy-start(bf16[384,1280]{1,0:T(8,128)(2,1)} %param.21) | copy-start | bytes 2949124
  7.2 48.7 %all-reduce.6.cloned.1.call-start = ((), (), s32[]{:S(2)}) async-start(), calls=%async_computation.1 | async-start | bytes 655360 | tf_op jit(solution)/shard_map/psum | solution.py:66
  12.3 49.0 %copy-start.7 = (bf16[2048]{0:T(1024)(128)(2,1)S(1)}, bf16[2048]{0:T(1024)(128)(2,1)}, u32[]{:S(2)}) copy-start(bf16[2048]{0:T(1024)(128)(2,1)} %param.23) | copy-start | bytes 12292
  16.6 79.7 %all-gather.5.cloned.1.call-start = ((), (), s32[]{:S(2)}) async-start(), calls=%async_computation.3 | async-start | bytes 1310720 | tf_op jit(solution)/shard_map/all_gather | solution.py:84
  56.9 27.9 %copy-start.2 = (bf16[64,1280]{1,0:T(8,128)(2,1)}, bf16[64,1280]{1,0:T(8,128)(2,1)S(1)}, u32[]{:S(2)}) copy-start(bf16[64,1280]{1,0:T(8,128)(2,1)S(1)} %add_convert_fusion) | copy-start | bytes 491524
  61.2 36.6 %all-gather.3.cloned.1.call-start = ((), (), s32[]{:S(2)}) async-start(), calls=%async_computation.2 | async-start | bytes 1310720 | tf_op jit(solution)/shard_map/all_gather | solution.py:83
  65.5 254.5 %all-reduce.4.cloned.1.call-start = ((), (), s32[]{:S(2)}) async-start(), calls=%async_computation | async-start | bytes 25165824 | tf_op jit(solution)/shard_map/psum | solution.py:74
  84.9 0.7 copy-start.5
  84.9 531.0 %all-reduce.8.cloned.1.call-start = ((), (), s32[]{:S(2)}) async-start(), calls=%async_computation.4 | async-start | bytes 12582912 | tf_op jit(solution)/shard_map/psum | solution.py:115
  392.6 0.7 copy-start.6
  615.9 12.6 %copy-start.1 = (bf16[1280,384]{1,0:T(8,128)(2,1)S(1)}, bf16[1280,384]{1,0:T(8,128)(2,1)}, u32[]{:S(2)}) copy-start(bf16[1280,384]{1,0:T(8,128)(2,1)} %param.19) | copy-start | bytes 2949124
Sparse Core Ops, SparseCore 0:
  16.7 39.1 all-reduce.5
  61.4 16.4 all-gather.4
  79.4 16.8 all-gather.2
  99.2 220.7 all-reduce.3
  392.8 223.0 all-reduce.7
where the time goes:
time: 636 us; the launch traced here: 635 us
  waiting for transfers between devices  483 us (76%)
  matrix products  70.9 us (11%)
  other arithmetic  32.4 us (5%)
  local copies, waits for them, and re-layouts  28.4 us (4%)
  between operations  14 us (2%)
  blocking collectives  6.37 us (1%)
    psum x1, waiting for transfers between devices, shards(): lax.psum(block_part.astype(jnp.bfloat16), 'tensor').astype(jnp.float32)  223 us
    psum x1, waiting for transfers between devices, shards(): squares, query_sum = lax.psum((squares, query_part), 'seq')  221 us
    psum x1, waiting for transfers between devices, shards(): latent_sum = lax.psum(partial_value, 'tensor')  39.3 us
    dot_general x1, matrix products, shards(): query_part = jnp.dot(scaled, wq_x, preferred_element_type=jnp.float32)  19.3 us
    dot_general x1, matrix products, shards(): block_part = jnp.dot(attended, wo_x, preferred_element_type=jnp.float32)  18.9 us
    unnamed x19, local copies, waits for them, and re-layouts  13.5 us
  transfers between devices with their start and end apart: 5, of which 3 were waited for; matrix products, arithmetic and copies ran while one was open for 5% of the time, Pallas kernels for 0%

commit v1 on v0

--- a/solution.py
+++ b/solution.py
@@ -112,7 +112,9 @@
     attended = lax.map(attend, (q_blocks, img_blocks)).reshape(tok_count, heads_x * HEAD)
     block_part = jnp.dot(attended, wo_x, preferred_element_type=jnp.float32)
     gate_open = jnp.tanh(gate_x)
-    block_whole = lax.psum(block_part.astype(jnp.bfloat16), "tensor").astype(jnp.float32)
+    block_whole = jnp.sum(lax.all_gather(block_part.astype(jnp.bfloat16), "tensor"), axis=0).astype(
+        jnp.float32
+    )
     text_out = hidden + gate_open * block_whole
     return (text_out, page_latents)
 

time: 636 us -> 856 us (1.35)
  waiting for transfers between devices: 483 us -> 685 us
  other arithmetic: 32.4 us -> 50.2 us
    all_gather x0 -> x1, waiting for transfers between devices: none -> 425 us  [shards(): lax.all_gather(block_part.astype(jnp.bfloat16), 'tensor')]
    psum x1 -> x0, waiting for transfers between devices: 223 us -> none  [shards(): lax.psum(block_part.astype(jnp.bfloat16), 'tensor').astype(jnp.float32)]
    reduce_sum x0 -> x1, other arithmetic: none -> 17.8 us  [shards(): jnp.sum(lax.all_gather(block_part.astype(jnp.bfloat16), 'tensor'), axis=0)]
  transfers between devices with their start and end apart: 5 -> 5, of which waited for: 3 -> 3; matrix products, arithmetic and copies ran while one was open for 5% -> 4% of each run, Pallas kernels for 0% -> 0%
where the time goes in v1:
time: 856 us; the launch traced here: 855 us
  waiting for transfers between devices  685 us (80%)
  matrix products  70.9 us (8%)
  other arithmetic  50.2 us (6%)
  local copies, waits for them, and re-layouts  28.4 us (3%)
  between operations  14 us (2%)
    all_gather x1, waiting for transfers between devices, shards(): lax.all_gather(block_part.astype(jnp.bfloat16), 'tensor')  425 us
    psum x1, waiting for transfers between devices, shards(): squares, query_sum = lax.psum((squares, query_part), 'seq')  221 us
    psum x1, waiting for transfers between devices, shards(): latent_sum = lax.psum(partial_value, 'tensor')  39.3 us
    dot_general x1, matrix products, shards(): query_part = jnp.dot(scaled, wq_x, preferred_element_type=jnp.float32)  19.3 us
    dot_general x1, matrix products, shards(): block_part = jnp.dot(attended, wo_x, preferred_element_type=jnp.float32)  18.9 us
    reduce_sum x1, other arithmetic, shards(): jnp.sum(lax.all_gather(block_part.astype(jnp.bfloat16), 'tensor'), axis=0)  17.8 us
  transfers between devices with their start and end apart: 5, of which 3 were waited for; matrix products, arithmetic and copies ran while one was open for 4% of the time, Pallas kernels for 0%

profile of v1, /device:TPU:0, one launch (start us, length us, event | category | flops | bytes accessed | tf_op | source)
XLA Modules:
  0.0 855.1 jit_solution(6373963777856643626)
XLA Ops:
  7.2 1.4 copy-done
  8.7 1.6 convolution_convert_fusion.4
  10.3 0.3 reshape.96
  10.6 1.6 convolution_convert_fusion.5
  12.3 1.9 convolution_convert_fusion.3
  14.2 0.3 reshape.99
  14.6 0.3 fusion.24
  14.9 0.2 convert_reduce_fusion.1
  15.1 0.3 fusion.19
  15.5 0.1 convert_element_type.88
  15.6 1.0 fusion.25
  16.7 39.3 %all-reduce.5.cloned.1.call-done = f32[64,1280]{1,0:T(8,128)} async-done(((f32[64,1280]{1,0:T(8,128)}), f32[64,1280]{1,0:T(8,128)}) %all-reduce.5.cloned.1.call-update) | async-done | bytes 327696 | tf_op jit(solution)/shard_map/psum | solution.py:66
  55.9 1.0 add_convert_fusion
  56.9 4.3 convolution_convert_fusion.1
  61.3 4.2 convolution_convert_fusion.2
  65.6 19.3 %fusion.12 = f32[1536,2048]{1,0:T(8,128)} fusion(bf16[2048,2048]{1,0:T(8,128)(2,1)} %param.24, bf16[1536,2048]{1,0:T(8,128)(2,1)} %param.22, f32[2048]{0:T(1024)S(1)} %convert_element_type.76), kind=kOutput, calls=%fused_computation.30 | convolution fusion | flops 12894339072 | bytes 27271168 | tf_op jit(solution)/shard_map/dot_general | solution.py:73
  84.9 0.6 copy-done.5
  85.6 4.3 fusion.10
  89.9 6.4 psum.22
  96.3 1.5 copy_bitcast_fusion.2
  97.8 1.5 copy_bitcast_fusion.3
  99.3 220.7 %all-reduce.3.cloned.1.call-done = f32[1536,2048]{1,0:T(8,128)} async-done(((f32[1536,2048]{1,0:T(8,128)}), f32[1536,2048]{1,0:T(8,128)}) %all-reduce.3.cloned.1.call-update) | async-done | bytes 12582928 | tf_op jit(solution)/shard_map/psum | solution.py:74
  320.0 8.4 fusion.11
  328.4 7.8 copy.39
  336.1 37.6 %while.11 = (s32[]{:T(128)}, bf16[3,512,16,128]{3,2,1,0:T(8,128)(2,1)}, s32[3,512]{1,0:T(4,128)S(1)}, bf16[3,512,16,128]{3,2,1,0:T(8,128)(2,1)}, bf16[256,16,128...) while((s32[]{:T(128)}, bf16[3,512,16,128]{3,2,1,0:T(8,128)(2,1)}, ...), condition=%wide.region_9.10_spmd.clone, body=%wide.region_6.9_spmd.clone.sunk | while | flops 1104268288 | bytes 40548948 | solution.py:112
  336.2 0.1 broadcast_compare_fusion.2
  336.3 2.0 constant_dynamic-slice_fusion.5
  338.3 2.4 fusion.50
  340.7 1.8 convert_reduce_fusion.3
  342.5 3.5 fusion.51
  346.0 2.7 copy_dynamic-update-slice_fusion.2
  348.7 0.1 broadcast_compare_fusion.2
  348.9 2.0 constant_dynamic-slice_fusion.5
  350.8 2.4 fusion.50
  353.2 1.8 convert_reduce_fusion.3
  355.1 3.5 fusion.51
  358.5 2.7 copy_dynamic-update-slice_fusion.2
  361.2 0.1 broadcast_compare_fusion.2
  361.4 2.0 constant_dynamic-slice_fusion.5
  363.3 2.4 fusion.50
  365.7 1.8 convert_reduce_fusion.3
  367.6 3.5 fusion.51
  371.0 2.7 copy_dynamic-update-slice_fusion.2
  373.8 18.9 %convolution_convert_fusion = bf16[1536,2048]{1,0:T(8,128)(2,1)} fusion(bf16[2048,2048]{1,0:T(8,128)(2,1)} %param.27, bf16[192,8,16,128]{3,2,1,0:T(8,128)(2,1)} %bitcast.21), kind=kOutput, calls=%fused_computation.28 | convolution fusion | flops 12888047616 | bytes 20971520 | tf_op jit(solution)/shard_map/dot_general | solution.py:113
  392.7 0.7 copy-done.6
  393.3 424.8 %all-gather.9.cloned.1.call-done = bf16[6144,2048]{1,0:T(8,128)(2,1)} async-done(((bf16[1536,2048]{1,0:T(8,128)(2,1)}), bf16[6144,2048]{1,0:T(8,128)(2,1)}) %all-gather.9.cloned.1.call-update) | async-done | bytes 25165840 | tf_op jit(solution)/shard_map/all_gather | solution.py:115
  818.2 17.8 %reduce_sum.41 = bf16[1536,2048]{1,0:T(8,128)(2,1)} reduce(bf16[4,1536,2048]{2,1,0:T(8,128)(2,1)} %bitcast.79, bf16[]{:T(256)} %constant.43.clone.1), dimensions={0}, to_apply=%region_10.11 | reduce | flops 9437184 | bytes 31457282 | tf_op jit(solution)/shard_map/reduce_sum | solution.py:115
  836.0 12.6 %convert_add_fusion = f32[1536,2048]{1,0:T(8,128)} fusion(bf16[1536,2048]{1,0:T(8,128)(2,1)} %param.22, bf16[1536,2048]{1,0:T(8,128)(2,1)} %reduce_sum.41, f32[2048]{0:T(1024)S(1)} %tanh.3), kind=kLoop, calls=%fused_computation.22 | loop fusion | flops 12582912 | bytes 25174016 | tf_op jit(solution)/shard_map/add | solution.py:118
  (41 shorter events, 0.6 us)
Async XLA Ops:
  7.2 1.5 copy-start
  7.2 48.7 %copy-start.4 = (bf16[64,1280]{1,0:T(8,128)(2,1)S(1)}, bf16[64,1280]{1,0:T(8,128)(2,1)}, u32[]{:S(2)}) copy-start(bf16[64,1280]{1,0:T(8,128)(2,1)} %param.17) | copy-start | bytes 491524
  7.2 8.4 copy-start.3
  7.2 48.7 %all-reduce.5.cloned.1.call-start = ((), (), s32[]{:S(2)}) async-start(), calls=%async_computation.1 | async-start | bytes 655360 | tf_op jit(solution)/shard_map/psum | solution.py:66
  12.3 49.0 %copy-start.7 = (bf16[2048]{0:T(1024)(128)(2,1)S(1)}, bf16[2048]{0:T(1024)(128)(2,1)}, u32[]{:S(2)}) copy-start(bf16[2048]{0:T(1024)(128)(2,1)} %param.23) | copy-start | bytes 12292
  16.6 79.7 %all-gather.7.cloned.1.call-start = ((), (), s32[]{:S(2)}) async-start(), calls=%async_computation.3 | async-start | bytes 1310720 | tf_op jit(solution)/shard_map/all_gather | solution.py:84
  56.9 27.9 %copy-start.2 = (bf16[64,1280]{1,0:T(8,128)(2,1)}, bf16[64,1280]{1,0:T(8,128)(2,1)S(1)}, u32[]{:S(2)}) copy-start(bf16[64,1280]{1,0:T(8,128)(2,1)S(1)} %add_convert_fusion) | copy-start | bytes 491524
  61.2 36.6 %all-gather.5.cloned.1.call-start = ((), (), s32[]{:S(2)}) async-start(), calls=%async_computation.2 | async-start | bytes 1310720 | tf_op jit(solution)/shard_map/all_gather | solution.py:83
  65.5 254.5 %all-reduce.3.cloned.1.call-start = ((), (), s32[]{:S(2)}) async-start(), calls=%async_computation | async-start | bytes 25165824 | tf_op jit(solution)/shard_map/psum | solution.py:74
  84.9 0.7 copy-start.5
  84.9 733.3 %all-gather.9.cloned.1.call-start = ((), (), s32[]{:S(2)}) async-start(), calls=%async_computation.4 | async-start | bytes 31457280 | tf_op jit(solution)/shard_map/all_gather | solution.py:115
  392.6 0.7 copy-start.6
  836.0 12.6 %copy-start.1 = (bf16[1280,384]{1,0:T(8,128)(2,1)S(1)}, bf16[1280,384]{1,0:T(8,128)(2,1)}, u32[]{:S(2)}) copy-start(bf16[1280,384]{1,0:T(8,128)(2,1)} %param.19) | copy-start | bytes 2949124
Sparse Core Ops, SparseCore 0:
  16.7 39.1 all-reduce.4
  61.4 16.4 all-gather.6
  79.4 16.8 all-gather.4
  99.2 220.7 all-reduce.2
  392.8 425.3 all-gather.8
